TPU v7x, 32 devices: a whole 2x2x4 slice. The times are simulated.
32 devices in a mesh: lat: 4 (over z), lon: 8 (over y, x, core).
Axes of the slice: x: 2, y: 2, z: 4, core: 2. Of those that a mesh axis runs over, the one named last changes fastest.
Arguments:
- fields: float32 [5, 960, 2880], P(None, 'lat', 'lon'), may hold values from -6 to 6
- east_courant: float32 [960, 2880], P('lat', 'lon'), may hold values from -0.4 to 0.4
- north_courant: float32 [960, 2880], P('lat', 'lon'), may hold values from -0.4 to 0.4
- cutoff: int32 [960], replicated, may hold values from 1 to 1439
- damping: float32 [960], replicated, may hold values from 0.05 to 0.5
- ship_rows: int32 [4, 4, 60], replicated, may hold values from -1 to 239, as said below
Outputs:
- updated: float32 [5, 960, 2880], P(None, 'lat', 'lon')
Inputs may be any that keep to these rules, and one draw needn't show every extreme that they name: ship_rows[s, d, j] is a row of band s (0 to 239) whose filter is computed by band d, or -1 for an empty slot; no row is listed twice; every row within 240 rows of either pole is listed, no row farther than 360 from both poles is listed, and rows between are listed or not, so that bands 0 and 3 are covered whole; a band's listed rows fill the slots of its destinations in full except the last destination it uses, so band 0 fills 60 slots to some band.
All inputs are finite; a program needn't handle non-finite values.
Results may differ from a plain program's by a relative error of at most 0.0003.
Values sent between devices are 32-bit elements; how exact they have to be, the bound alone decides.
A program may use at most 256 MiB of HBM per device.

v0:
```python
import math

import jax
import jax.numpy as jnp
from jax import lax
from jax.sharding import PartitionSpec as P

HIGHEST_PRECISION = lax.Precision.HIGHEST


def with_halo(cells, sides, width, closed):
    for axis, dim in sides:
        count = lax.axis_size(axis)
        ends = count if closed else count - 1
        head = lax.slice_in_dim(cells, 0, width, axis=dim)
        tail = lax.slice_in_dim(cells, cells.shape[dim] - width, cells.shape[dim], axis=dim)
        cells = jnp.concatenate(
            [
                lax.ppermute(tail, axis, [(i, (i + 1) % count) for i in range(ends)]),
                cells,
                lax.ppermute(head, axis, [((i + 1) % count, i) for i in range(ends)]),
            ],
            axis=dim,
        )
    return cells


def phase_pair(cutoffs, positions, length):
    turned = (2 * cutoffs[:, None] + 1) * positions[None, :] % (2 * length)
    angles = turned.astype(jnp.float32) * (math.pi / length)
    return (jnp.cos(angles), jnp.sin(angles))


def kernel_block(sources, targets, length):
    offsets = targets[None, :] - sources[:, None]
    magnitude = jnp.abs(offsets)
    nearest = jnp.minimum(magnitude, length - magnitude)
    nonzero = jnp.where(nearest == 0, 1, nearest)
    values = jnp.sign(offsets).astype(jnp.float32) / (
        length * jnp.sin(nonzero.astype(jnp.float32) * (math.pi / length))
    )
    return jnp.where(offsets == 0, jnp.float32(0.0), values)


def modulated_sum(running, column_piece, cutoffs, targets, length):
    piece_count = column_piece.shape[2]
    sources = jnp.arange(piece_count, dtype=jnp.int32)
    cos_part, sin_part = phase_pair(cutoffs, sources, length)
    stacked = jnp.stack([column_piece * cos_part[:, None, :], column_piece * sin_part[:, None, :]])
    flattened = stacked.reshape(-1, piece_count)
    kernel = kernel_block(sources, targets, length)
    product = jnp.dot(
        flattened, kernel, precision=HIGHEST_PRECISION, preferred_element_type=jnp.float32
    )
    return product.reshape(running.shape)


def finish_filter(running, local_rows, cutoffs, targets, damping_rows, length):
    cos_part, sin_part = phase_pair(cutoffs, targets, length)
    centre = (2 * cutoffs + 1).astype(jnp.float32) / length
    lowpass = (
        sin_part[:, None, :] * running[0]
        - cos_part[:, None, :] * running[1]
        + centre[:, None, None] * local_rows
    )
    return damping_rows[:, None, None] * local_rows + (1.0 - damping_rows[:, None, None]) * lowpass


def table_lookup(lookup_table, indices):
    matches = indices[:, None] == jnp.arange(lookup_table.shape[0], dtype=jnp.int32)[None, :]
    return jnp.sum(
        jnp.where(matches, lookup_table[None, :], jnp.zeros_like(lookup_table)[None, :]), axis=1
    )


def per_device(fields, east_courant, north_courant, cutoff, damping, ship_rows):
    channel_count, rows_dev, cols_dev = fields.shape
    band_count = lax.axis_size("lat")
    segment_count = lax.axis_size("lon")
    lat_count = rows_dev * band_count
    lon_count = cols_dev * segment_count
    band_index = lax.axis_index("lat")
    segment_index = lax.axis_index("lon")
    zonal = with_halo(jnp.concatenate([fields, east_courant[None]], axis=0), (("lon", 2),), 1, True)
    meridional = with_halo(
        jnp.concatenate([fields, north_courant[None]], axis=0), (("lat", 1),), 1, False
    )
    east_cells = zonal[:channel_count, :, 2:]
    west_cells = zonal[:channel_count, :, :-2]
    west_courant = zonal[channel_count, :, :-2]
    east_flux = east_courant * jnp.where(east_courant > 0, fields, east_cells)
    west_flux = west_courant * jnp.where(west_courant > 0, west_cells, fields)
    global_rows = band_index * rows_dev + jnp.arange(rows_dev, dtype=jnp.int32)
    latitudes = global_rows.astype(jnp.float32)
    face_n = jnp.sin((latitudes + 1.0) * (math.pi / lat_count))
    face_s = jnp.sin(latitudes * (math.pi / lat_count))
    centre = jnp.sin((latitudes + 0.5) * (math.pi / lat_count))
    north_mask = (global_rows < lat_count - 1).astype(jnp.float32)
    south_mask = (global_rows > 0).astype(jnp.float32)
    north_cells = meridional[:channel_count, 2:, :]
    south_cells = meridional[:channel_count, :-2, :]
    south_courant = meridional[channel_count, :-2, :]
    north_flux = (
        north_courant
        * jnp.where(north_courant > 0, fields, north_cells)
        * (face_n * north_mask)[:, None]
    )
    south_flux = (
        south_courant
        * jnp.where(south_courant > 0, south_cells, fields)
        * (face_s * south_mask)[:, None]
    )
    advected = fields - (east_flux - west_flux) - (north_flux - south_flux) / centre[:, None]
    outgoing_rows = lax.dynamic_index_in_dim(ship_rows, band_index, axis=0, keepdims=False).reshape(
        -1
    )
    outgoing_valid = outgoing_rows >= 0
    picked = jnp.take(advected, jnp.maximum(outgoing_rows, 0), axis=1)
    picked = jnp.where(outgoing_valid[None, :, None], picked, jnp.float32(0.0)).transpose(1, 0, 2)
    slot_count = picked.shape[0]
    arrived = lax.all_to_all(
        picked.reshape(band_count, -1, channel_count, cols_dev),
        "lat",
        split_axis=0,
        concat_axis=0,
        tiled=True,
    )
    arrived = arrived.reshape(slot_count, channel_count, cols_dev)
    incoming_rows = lax.dynamic_index_in_dim(ship_rows, band_index, axis=1, keepdims=False).reshape(
        -1
    )
    capacity = slot_count // band_count
    source_band = jnp.arange(slot_count, dtype=jnp.int32) // capacity
    incoming_global = jnp.where(incoming_rows >= 0, source_band * rows_dev + incoming_rows, 0)
    cutoffs = table_lookup(cutoff, incoming_global)
    damping_rows = table_lookup(damping, incoming_global)
    targets = segment_index * cols_dev + jnp.arange(cols_dev, dtype=jnp.int32)
    initial = jnp.zeros((2,) + arrived.shape, jnp.float32)
    running = modulated_sum(
        initial, lax.all_gather(arrived, "lon", axis=2, tiled=True), cutoffs, targets, lon_count
    )
    filtered = finish_filter(running, arrived, cutoffs, targets, damping_rows, lon_count)
    returned = lax.all_to_all(
        filtered.reshape(band_count, -1, channel_count, cols_dev),
        "lat",
        split_axis=0,
        concat_axis=0,
        tiled=True,
    )
    returned = returned.reshape(slot_count, channel_count, cols_dev)
    placement = jnp.where(outgoing_valid, outgoing_rows, rows_dev)
    return advected.at[:, placement, :].set(returned.transpose(1, 0, 2), mode="drop")


def solution(mesh):
    placed = (P(None, "lat", "lon"), P("lat", "lon"), P("lat", "lon"), P(), P(), P())
    return jax.shard_map(
        per_device, mesh=mesh, in_specs=placed, out_specs=P(None, "lat", "lon"), check_vma=False
    )
```

profile of v0, /device:TPU:0, one launch (start us, length us, event | category | flops | bytes accessed | tf_op | source)
XLA Modules:
  0.0 518.8 jit_solution(7479676274369579383)
XLA Ops:
  6.5 2.3 copy.66
  9.8 4.9 collective-permute-start.3
  17.4 2.0 copy.63
  20.7 2.7 collective-permute-start
  32.0 1.8 copy.64
  33.8 1.8 maximum_bitcast_fusion
  35.6 1.7 fusion.52
  37.3 1.9 copy.62
  39.2 4.4 fusion.42
  44.6 5.1 fusion.23
  49.7 2.6 gather_fusion
  54.0 50.3 %all_to_all.10 = f32[4,60,5,360]{3,1,2,0:T(8,128)S(1)} all-to-all(f32[4,60,5,360]{3,1,2,0:T(8,128)S(1)} %copy.69), channel_id=1, replica_groups=mesh['lat'=4,'lon'=8] {'lat'}, dimensions={0} | all-to-all | bytes 3456000 | tf_op jit(solution)/shard_map/all_to_all | solution.py:121
  104.3 3.6 copy.81
  107.9 5.2 %reshape.289 = f32[240,5,360]{0,1,2:T(8,128)} reshape(f32[4,60,5,360]{1,0,2,3:T(4,128)} %copy.81) | data formatting | bytes 3456000 | tf_op jit(solution)/shard_map/reshape | solution.py:128
  114.7 1.7 fusion.50
  116.4 13.7 %fusion.30 = (f32[240,2880]{0,1:T(8,128)}, f32[240,2880]{0,1:T(8,128)}) fusion(s32[240]{0:T(256)S(1)} %multiply_add_fusion), kind=kLoop, calls=%fused_computation.45 | loop fusion | flops 6220800 | bytes 5530560 | tf_op jit(solution)/shard_map/cos | solution.py:31
  130.1 18.3 %fusion.66 = f32[2880,360]{1,0:T(8,128)} fusion(s32[360]{0:T(512)S(1)} %iota_add_fusion), kind=kLoop, calls=%fused_computation.12.clone.clone.1 | loop fusion | flops 14515200 | bytes 4148640 | tf_op jit(solution)/shard_map/dot_general | solution.py:52
  148.4 81.8 %all-gather.2.cloned.1.call-done = f32[240,5,2880]{0,1,2:T(8,128)} async-done(((f32[240,5,360]{0,1,2:T(8,128)}), f32[240,5,2880]{0,1,2:T(8,128)}) %all-gather.2.cloned.1.call-update) | async-done | bytes 13824016 | tf_op jit(solution)/shard_map/all_gather | solution.py:140
  230.1 26.0 %multiply_bitcast_fusion.1 = (f32[1,240,5,2880]{1,2,3,0:T(8,128)}, f32[1,240,5,2880]{1,2,3,0:T(8,128)}) fusion(f32[240,5,2880]{0,1,2:T(8,128)} %all-gather.2.cloned.1.call-done, f32[240,2880]{0,1:T(8,128)} %get-tuple-element.17, f32[240,2880]{0,1:T(8,128)} %get-tuple-element.18), kind=kLoop, calls=%fused_computation.4 | loop fusion | flops 6912000 | bytes 47001600 | tf_op jit(solution)/shard_map/stack | solution.py:49
  256.1 34.0 %pad_maximum_fusion = f32[2,240,5,2880]{1,2,3,0:T(8,128)} fusion(f32[1,240,5,2880]{1,2,3,0:T(8,128)} %get-tuple-element.8, f32[1,240,5,2880]{1,2,3,0:T(8,128)} %get-tuple-element.7), kind=kLoop, calls=%fused_computation.2 | loop fusion | flops 6912000 | bytes 55296000 | tf_op jit(solution)/shard_map/stack | solution.py:49
  290.1 47.7 %copy.73 = f32[2,240,5,2880]{3,2,1,0:T(8,128)} copy(f32[2,240,5,2880]{1,2,3,0:T(8,128)} %pad_maximum_fusion) | data formatting | bytes 55296000 | tf_op jit(solution)/shard_map/stack | solution.py:49
  337.8 35.2 %reshape.271 = f32[2400,2880]{1,0:T(8,128)} reshape(f32[2,240,5,2880]{3,2,1,0:T(8,128)} %copy.73) | data formatting | bytes 55296000 | tf_op jit(solution)/shard_map/reshape | solution.py:50
  373.0 43.7 %fusion.6 = f32[2400,360]{0,1:T(8,128)S(1)} fusion(f32[2400,2880]{1,0:T(8,128)} %reshape.271, f32[2880,360]{1,0:T(8,128)} %fusion.66), kind=kOutput, calls=%fused_computation.13 | convolution fusion | flops 29859840000 | bytes 35251200 | tf_op jit(solution)/shard_map/dot_general | solution.py:52
  416.7 2.4 fusion.61
  419.2 2.8 copy.75
  422.0 3.1 squeeze.13
  425.0 2.8 copy.74
  427.8 3.1 squeeze.12
  430.9 4.7 fusion.13
  436.0 50.2 %all_to_all.11 = f32[4,60,5,360]{3,1,2,0:T(8,128)S(1)} all-to-all(f32[4,60,5,360]{3,1,2,0:T(8,128)S(1)} %copy.77), channel_id=1, replica_groups=mesh['lat'=4,'lon'=8] {'lat'}, dimensions={0} | all-to-all | bytes 3456000 | tf_op jit(solution)/shard_map/all_to_all | solution.py:143
  486.2 2.7 copy.82
  488.9 21.5 %scatter_fusion = f32[5,240,360]{2,0,1:T(8,128)S(1)} fusion(f32[5,240,360]{2,0,1:T(8,128)S(1)} %copy-done, s32[240]{0:T(256)S(1)} %bitcast.30, f32[240,5,360]{2,1,0:T(8,128)} %bitcast.28), kind=kCustom, calls=%fused_computation.1 | custom fusion | bytes 5184960 | tf_op jit(solution)/shard_map/scatter | solution.py:152
  (70 shorter events, 19.5 us)
Async XLA Ops:
  6.5 223.6 %all-gather.2.cloned.1.call-start = ((), (), s32[]{:S(2)}) async-start(), calls=%async_computation.2 | async-start | bytes 26542080 | tf_op jit(solution)/shard_map/all_gather | solution.py:140
  6.5 2.3 copy-start.5
  8.9 7.2 %copy-start.1 = (f32[5,240,360]{2,1,0:T(8,128)S(1)}, f32[5,240,360]{2,1,0:T(8,128)}, u32[]{:S(2)}) copy-start(f32[5,240,360]{2,1,0:T(8,128)} %param.6) | copy-start | bytes 5184004
  8.9 7.2 %copy-start.2 = (f32[240,360]{1,0:T(8,128)S(1)}, f32[240,360]{1,0:T(8,128)}, u32[]{:S(2)}) copy-start(f32[240,360]{1,0:T(8,128)} %param.7) | copy-start | bytes 1036804
  9.1 8.2 %copy-start.3 = (f32[1,240,360]{2,0,1:T(1,128)}, f32[1,240,360]{2,0,1:T(1,128)S(1)}, u32[]{:S(2)}) copy-start(f32[1,240,360]{2,0,1:T(1,128)S(1)} %broadcast_in_dim.115) | copy-start | bytes 1036804
  9.8 33.8 %collective-permute-start.3 = (f32[6,1,360]{2,0,1:T(8,128)}, f32[6,1,360]{2,0,1:T(8,128)S(1)}, u32[]{:S(2)}, u32[]{:S(2)}) collective-permute-start(f32[6,1,360]{2,0,1:T(8,128)} %get-tuple-element.12), channel_id=1, source_target_pairs={{0,8},{8,16},{16,24},{1,9},{9,17},{17,25},{2,10},{10,18},{18,26},{... | collective-permute-start | bytes 25928 | tf_op jit(solution)/shard_map/ppermute | solution.py:19
  14.7 29.7 %collective-permute-start.2 = (f32[6,1,360]{2,0,1:T(8,128)S(1)}, f32[6,1,360]{2,0,1:T(8,128)S(1)}, u32[]{:S(2)}, u32[]{:S(2)}) collective-permute-start(f32[6,1,360]{2,0,1:T(8,128)S(1)} %get-tuple-element.11), channel_id=1, source_target_pairs={{8,0},{16,8},{24,16},{9,1},{17,9},{25,17},{10,2},{18,10},{26,18},{... | collective-permute-start | bytes 25928 | tf_op jit(solution)/shard_map/ppermute | solution.py:21
  19.4 12.6 %collective-permute-start.1 = (f32[6,240,1]{1,2,0:T(1,128)}, f32[6,240,1]{1,2,0:T(1,128)}, u32[]{:S(2)}, u32[]{:S(2)}) collective-permute-start(f32[6,240,1]{1,2,0:T(1,128)} %copy.63), channel_id=1, source_target_pairs={{0,1},{1,2},{2,3},{3,4},{4,5},{5,6},{6,7},{7,0},{8,9},{9,10},{10,1... | collective-permute-start | bytes 17288 | tf_op jit(solution)/shard_map/ppermute | solution.py:19
  20.7 16.6 %collective-permute-start = (f32[6,240,1]{1,2,0:T(1,128)S(1)}, f32[6,240,1]{1,2,0:T(1,128)}, u32[]{:S(2)}, u32[]{:S(2)}) collective-permute-start(f32[6,240,1]{1,2,0:T(1,128)S(1)} %copy.61), channel_id=1, source_target_pairs={{1,0},{2,1},{3,2},{4,3},{5,4},{6,5},{7,6},{0,7},{9,8},{10,9},{11,1... | collective-permute-start | bytes 17288 | tf_op jit(solution)/shard_map/ppermute | solution.py:21
  39.2 4.4 copy-start.4
  43.6 1.0 copy-start.6
  43.6 1.0 copy-start.8
  43.6 1.0 copy-start.9
  43.6 1.0 copy-start.12
  49.7 2.6 copy-start.13
  49.7 2.6 copy-start.14
  113.1 0.9 copy-start.10
  113.1 1.2 copy-start.11
  486.2 2.7 copy-start
  486.2 2.7 copy-start.7
Sparse Core Ops, SparseCore 0:
  113.3 116.7 all-gather.1
where the time goes:
time: 522 us; the launch traced here: 519 us
  local copies, waits for them, and re-layouts  149 us (29%)
  other arithmetic  121 us (23%)
  blocking collectives  100 us (19%)
  waiting for transfers between devices  81.8 us (16%)
  matrix products  43.7 us (8%)
  between operations  13.7 us (3%)
  starting transfers between devices  8.91 us (2%)
    all_gather x1, waiting for transfers between devices, per_device(): lax.all_gather(arrived, 'lon', axis=2, tiled=True)  81.8 us
    another operation x2, other arithmetic, modulated_sum(): jnp.stack([column_piece * cos_part[:, None, :], column_piece * sin_part[:...  60 us
    all_to_all x1, blocking collectives, per_device(): lax.all_to_all(picked.reshape(band_count, -1, channel_count, cols_dev), '...  50.3 us
    all_to_all x1, blocking collectives, per_device(): lax.all_to_all(filtered.reshape(band_count, -1, channel_count, cols_dev),...  50.2 us
    another operation x1, local copies, waits for them, and re-layouts, modulated_sum(): jnp.stack([column_piece * cos_part[:, None, :], column_piece * sin_part[:...  47.7 us
    dot_general x1, matrix products, modulated_sum(): jnp.dot(flattened, kernel, precision=HIGHEST_PRECISION, preferred_element...  43.7 us
    reshape x1, local copies, waits for them, and re-layouts, modulated_sum(): flattened = stacked.reshape(-1, piece_count)  35.2 us
    scatter x2, local copies, waits for them, and re-layouts, per_device(): advected.at[:, placement, :].set(returned.transpose(1, 0, 2), mode='drop')  23 us
  transfers between devices with their start and end apart: 5, of which 1 were waited for; matrix products, arithmetic and copies ran while one was open for 12% of the time, Pallas kernels for 0%

commit v1 on v0

v1 whole, which is shorter than its diff:
```python
import functools
import math

import jax
import jax.numpy as jnp
import numpy as np
from jax import lax
from jax.experimental import pallas as pl
from jax.experimental.pallas import tpu as pltpu
from jax.sharding import PartitionSpec as P

MESH = pl.DeviceIdType.MESH
BF16 = jnp.bfloat16


def ceil_to(value, unit):
    return -(-value // unit) * unit


def chunk_rows(total, pieces):
    tiles = total // 8
    pieces = min(pieces, tiles)
    sizes = [8 * (tiles // pieces + (1 if i < tiles % pieces else 0)) for i in range(pieces)]
    return [(sum(sizes[:i]), sizes[i]) for i in range(pieces)]


def tables(segments, length, width):
    index = np.arange(length, dtype=np.int64)
    angle = (index[:, None] * index[None, :] % length) * (2 * math.pi / length)
    matrix = np.zeros((width, 2 * width), np.float64)
    matrix[:length, :length] = np.cos(angle)
    matrix[:length, width : width + length] = np.sin(angle)
    hi = matrix.astype(np.float32).astype(BF16)
    lo = (matrix - hi.astype(np.float64)).astype(np.float32).astype(BF16)
    stacked = np.concatenate([hi, hi, lo], axis=0)
    half = segments // 2
    twiddle = np.zeros((2 * (half + 1), width), np.float64)
    for residue in range(half + 1):
        turn = (residue * index % (segments * length)) * (2 * math.pi / (segments * length))
        twiddle[2 * residue, :length] = np.cos(turn)
        twiddle[2 * residue + 1, :length] = np.sin(turn)
    return stacked, twiddle.astype(np.float32)


def real_dft(parts):
    count = len(parts)
    if count == 1:
        return [(parts[0], None)]
    if count == 2:
        return [(parts[0] + parts[1], None), (parts[0] - parts[1], None)]
    half, quarter = count // 2, count // 4
    even, odd = real_dft(parts[0::2]), real_dft(parts[1::2])
    spectrum = [None] * (half + 1)
    for k in range(quarter + 1):
        er, ei = even[k]
        orr, oi = odd[k]
        if k == 0:
            spectrum[0] = (er + orr, None)
            spectrum[half] = (er - orr, None)
        elif k == quarter:
            spectrum[k] = (er, -orr)
        else:
            c, s = math.cos(2 * math.pi * k / count), math.sin(2 * math.pi * k / count)
            tr = c * orr + s * oi
            ti = c * oi - s * orr
            spectrum[k] = (er + tr, ei + ti)
            spectrum[half - k] = (er - tr, ti - ei)
    return spectrum


def real_idft(spectrum):
    half = len(spectrum) - 1
    count = 2 * half
    if count == 2:
        a, b = spectrum[0][0], spectrum[1][0]
        return [a + b, a - b]
    quarter = half // 2
    even, odd = [None] * (quarter + 1), [None] * (quarter + 1)
    for k in range(quarter + 1):
        if k == 0:
            a, b = spectrum[0][0], spectrum[half][0]
            even[0], odd[0] = (a + b, None), (a - b, None)
        elif k == quarter:
            a, b = spectrum[k]
            even[k], odd[k] = (2.0 * a, None), (-2.0 * b, None)
        else:
            ar, ai = spectrum[k]
            br, bi = spectrum[half - k]
            even[k] = (ar + br, ai - bi)
            dr, di = ar - br, ai + bi
            c, s = math.cos(2 * math.pi * k / count), math.sin(2 * math.pi * k / count)
            odd[k] = (c * dr - s * di, s * dr + c * di)
    out = [None] * count
    out[0::2] = real_idft(even)
    out[1::2] = real_idft(odd)
    return out


def filter_rows(parts, cut, damp, weight, twiddle, spread, length):
    segments = len(parts)
    half = segments // 2
    rows, width = parts[0].shape
    total = segments * length
    stride = ceil_to(rows, 16)
    slots = 0

    def put(value):
        nonlocal slots
        hi = value.astype(BF16)
        lo = (value - hi.astype(jnp.float32)).astype(BF16)
        here = pl.ds(slots * stride, rows)
        spread[here, 0:width] = hi
        spread[here, width : 2 * width] = lo
        spread[here, 2 * width : 3 * width] = hi
        slots += 1
        return slots - 1

    def multiply():
        return jnp.dot(
            spread[0 : slots * stride, :], weight[...], preferred_element_type=jnp.float32
        )

    def pick(product, slot, which):
        return product[slot * stride : slot * stride + rows, which * width : (which + 1) * width]

    places = []
    for k, (re, im) in enumerate(real_dft(parts)):
        if k == 0:
            places.append((put(re), None))
            continue
        c, s = twiddle[2 * k : 2 * k + 1, :], twiddle[2 * k + 1 : 2 * k + 2, :]
        if im is None:
            places.append((put(re * c), put(-(re * s))))
        else:
            places.append((put(re * c + im * s), put(im * c - re * s)))
    product = multiply()
    slots = 0
    scale = 1.0 / total
    pass_band = jnp.float32(scale)
    stop_band = damp * jnp.float32(scale)
    lane = lax.broadcasted_iota(jnp.int32, (rows, width), 1)
    back = []
    for k, (a, b) in enumerate(places):
        wave = k + segments * lane
        response = jnp.where(jnp.minimum(wave, total - wave) <= cut, pass_band, stop_band)
        re, im = pick(product, a, 0), -pick(product, a, 1)
        if b is not None:
            re, im = re + pick(product, b, 1), im + pick(product, b, 0)
        back.append((put(re * response), put(im * response)))
    product = multiply()
    spectrum = []
    for k, (a, b) in enumerate(back):
        re = pick(product, a, 0) - pick(product, b, 1)
        if k == 0:
            spectrum.append((re, None))
            continue
        im = pick(product, b, 0) + pick(product, a, 1)
        c, s = twiddle[2 * k : 2 * k + 1, :], twiddle[2 * k + 1 : 2 * k + 2, :]
        if k == half:
            spectrum.append((re * c - im * s, None))
        else:
            spectrum.append((re * c - im * s, im * c + re * s))
    return real_idft(spectrum)


def filter_kernel(
    segments, length, chunks,
    advected, cut_ref, damp_ref, weight, twiddle, out_ref,
    gathered, results, spread, send_a, recv_a, send_b, recv_b,
):
    me = lax.axis_index("lon")
    peers = [lax.rem(me + p, segments) for p in range(1, segments)]
    barrier = pltpu.get_barrier_semaphore()
    for peer in peers:
        pl.semaphore_signal(barrier, inc=1, device_id={"lon": peer}, device_id_type=MESH)
    pl.semaphore_wait(barrier, segments - 1)
    outward, homeward = [], []
    for c, (start, rows) in enumerate(chunks):
        window = pl.ds(start, rows)
        for p, peer in enumerate(peers):
            copy = pltpu.make_async_remote_copy(
                src_ref=advected.at[peer, window],
                dst_ref=gathered.at[me, window],
                send_sem=send_a.at[c, p],
                recv_sem=recv_a.at[c, p],
                device_id={"lon": peer},
                device_id_type=MESH,
            )
            copy.start()
            outward.append(copy)
    for c, (start, rows) in enumerate(chunks):
        window = pl.ds(start, rows)
        gathered[me, window] = advected[me, window]
        for p in range(segments - 1):
            outward[c * (segments - 1) + p].wait_recv()
        filtered = filter_rows(
            [gathered[j, window] for j in range(segments)],
            cut_ref[window, :], damp_ref[window, :], weight, twiddle, spread, length,
        )
        for j in range(segments):
            results[j, window] = filtered[j]
        for p, peer in enumerate(peers):
            copy = pltpu.make_async_remote_copy(
                src_ref=results.at[peer, window],
                dst_ref=out_ref.at[me, window],
                send_sem=send_b.at[c, p],
                recv_sem=recv_b.at[c, p],
                device_id={"lon": peer},
                device_id_type=MESH,
            )
            copy.start()
            homeward.append(copy)
        out_ref[me, window] = results[me, window]
    for copy in outward:
        copy.wait_send()
    for copy in homeward:
        copy.wait()


def circle_filter(advected, cut_rows, damp_rows, pieces=3):
    segments = lax.axis_size("lon")
    channels, rows_dev, length = advected.shape
    width = ceil_to(length, 128)
    share = ceil_to(ceil_to(channels * rows_dev, segments) // segments, 8)
    padded = share * segments
    chunks = chunk_rows(share, pieces)
    weight, twiddle = tables(segments, length, width)
    slots = segments + 2
    flat = jnp.pad(
        advected.reshape(channels * rows_dev, length),
        ((0, padded - channels * rows_dev), (0, width - length)),
    ).reshape(segments, share, width)
    me = lax.axis_index("lon")

    def mine(values):
        column = jnp.pad(jnp.tile(values, channels), (0, padded - channels * rows_dev))
        return lax.dynamic_slice_in_dim(column, me * share, share)[:, None]

    depth = slots * ceil_to(max(rows for _, rows in chunks), 16)
    semaphores = pltpu.SemaphoreType.DMA((len(chunks), segments - 1))
    filtered = pl.pallas_call(
        functools.partial(filter_kernel, segments, length, chunks),
        out_shape=jax.ShapeDtypeStruct((segments, share, width), jnp.float32),
        in_specs=[pl.BlockSpec(memory_space=pltpu.VMEM)] * 5,
        out_specs=pl.BlockSpec(memory_space=pltpu.VMEM),
        scratch_shapes=[
            pltpu.VMEM((segments, share, width), jnp.float32),
            pltpu.VMEM((segments, share, width), jnp.float32),
            pltpu.VMEM((depth, 3 * width), BF16),
            semaphores, semaphores, semaphores, semaphores,
        ],
        compiler_params=pltpu.CompilerParams(
            collective_id=0, has_side_effects=True, vmem_limit_bytes=56 * 1024 * 1024
        ),
    )(flat, mine(cut_rows), mine(damp_rows), jnp.asarray(weight), jnp.asarray(twiddle))
    return filtered.reshape(padded, width)[: channels * rows_dev, :length].reshape(advected.shape)


def shifted(cells, axis, step, closed):
    count = lax.axis_size(axis)
    pairs = [(i, (i + step) % count) for i in range(count) if closed or 0 <= i + step < count]
    return lax.ppermute(cells, axis, pairs)


def per_device(fields, east_courant, north_courant, cutoff, damping, ship_rows):
    channels, rows_dev, length = fields.shape
    bands = lax.axis_size("lat")
    lat_count = rows_dev * bands
    band = lax.axis_index("lat")
    stacked_east = jnp.concatenate([fields[:, :, -1], east_courant[None, :, -1]], axis=0)
    west_edge = shifted(stacked_east, "lon", 1, True)
    east_edge = shifted(fields[:, :, 0], "lon", -1, True)
    stacked_north = jnp.concatenate([fields[:, -1, :], north_courant[None, -1, :]], axis=0)
    south_edge = shifted(stacked_north, "lat", 1, False)
    north_edge = shifted(fields[:, 0, :], "lat", -1, False)
    east_cells = jnp.concatenate([fields[:, :, 1:], east_edge[:, :, None]], axis=2)
    west_cells = jnp.concatenate([west_edge[:channels, :, None], fields[:, :, :-1]], axis=2)
    west_courant = jnp.concatenate([west_edge[channels, :, None], east_courant[:, :-1]], axis=1)
    north_cells = jnp.concatenate([fields[:, 1:, :], north_edge[:, None, :]], axis=1)
    south_cells = jnp.concatenate([south_edge[:channels, None, :], fields[:, :-1, :]], axis=1)
    south_courant = jnp.concatenate([south_edge[channels, None, :], north_courant[:-1]], axis=0)
    east_flux = east_courant * jnp.where(east_courant > 0, fields, east_cells)
    west_flux = west_courant * jnp.where(west_courant > 0, west_cells, fields)
    global_rows = band * rows_dev + jnp.arange(rows_dev, dtype=jnp.int32)
    latitudes = global_rows.astype(jnp.float32)
    face_n = jnp.sin((latitudes + 1.0) * (math.pi / lat_count))
    face_s = jnp.sin(latitudes * (math.pi / lat_count))
    centre = jnp.sin((latitudes + 0.5) * (math.pi / lat_count))
    face_n = jnp.where(global_rows < lat_count - 1, face_n, 0.0)
    face_s = jnp.where(global_rows > 0, face_s, 0.0)
    north_flux = north_courant * jnp.where(north_courant > 0, fields, north_cells) * face_n[:, None]
    south_flux = south_courant * jnp.where(south_courant > 0, south_cells, fields) * face_s[:, None]
    advected = fields - (east_flux - west_flux) - (north_flux - south_flux) / centre[:, None]
    cut_rows = lax.dynamic_slice_in_dim(cutoff, band * rows_dev, rows_dev)
    damp_rows = lax.dynamic_slice_in_dim(damping, band * rows_dev, rows_dev)
    listed = lax.dynamic_index_in_dim(ship_rows, band, axis=0, keepdims=False).reshape(-1)
    polar = jnp.any(listed[:, None] == jnp.arange(rows_dev, dtype=jnp.int32)[None, :], axis=0)
    filtered = circle_filter(advected, cut_rows, damp_rows)
    return jnp.where(polar[None, :, None], filtered, advected)


def solution(mesh):
    placed = (P(None, "lat", "lon"), P("lat", "lon"), P("lat", "lon"), P(), P(), P())
    return jax.shard_map(
        per_device, mesh=mesh, in_specs=placed, out_specs=P(None, "lat", "lon"), check_vma=False
    )
```

time: 522 us -> 85.2 us (0.16)
  local copies, waits for them, and re-layouts: 149 us -> 18.2 us
  other arithmetic: 121 us -> 9.29 us
  blocking collectives: 100 us -> 0 us
  waiting for transfers between devices: 81.8 us -> 0.01 us
  Pallas kernels: 0 us -> 47.3 us
  matrix products: 43.7 us -> 0 us
  between operations: 13.7 us -> 0.22 us
    all_to_all x2 -> x0, blocking collectives: 100 us -> none  [the longest x1 50.3 us: per_device(): lax.all_to_all(picked.reshape(band_count, -1, channel_count, cols_dev), '...]
    all_gather x1 -> x0, waiting for transfers between devices: 81.8 us -> none  [per_device(): lax.all_gather(arrived, 'lon', axis=2, tiled=True)]
    another operation x2 -> x0, other arithmetic: 60 us -> none  [modulated_sum(): jnp.stack([column_piece * cos_part[:, None, :], column_piece * sin_part[:...]
    reshape x7 -> x0, local copies, waits for them, and re-layouts: 47.9 us -> none  [the longest x1 35.2 us: modulated_sum(): flattened = stacked.reshape(-1, piece_count)]
    another operation x1 -> x6, local copies, waits for them, and re-layouts: 47.7 us -> 0.3 us  [the longest x4 0.16 us: mine(): jnp.tile(values, channels)]
    pallas_call x0 -> x1, Pallas kernels: none -> 47.3 us  [circle_filter(): pl.pallas_call(functools.partial(filter_kernel, segments, length, chunks)...]
    dot_general x1 -> x0, matrix products: 43.7 us -> none  [modulated_sum(): jnp.dot(flattened, kernel, precision=HIGHEST_PRECISION, preferred_element...]
    scatter x2 -> x0, local copies, waits for them, and re-layouts: 23 us -> none  [per_device(): advected.at[:, placement, :].set(returned.transpose(1, 0, 2), mode='drop')]
  transfers between devices with their start and end apart: 5 -> 4, of which waited for: 1 -> 0; matrix products, arithmetic and copies ran while one was open for 12% -> 17% of each run, Pallas kernels for 0% -> 0%
where the time goes in v1:
time: 85.2 us; the launch traced here: 83.7 us
  Pallas kernels  47.3 us (56%)
  local copies, waits for them, and re-layouts  18.2 us (21%)
  other arithmetic  9.29 us (11%)
  starting transfers between devices  8.68 us (10%)
    pallas_call x1, Pallas kernels, circle_filter(): pl.pallas_call(functools.partial(filter_kernel, segments, length, chunks)...  47.3 us
    ppermute x4, starting transfers between devices, shifted(): return lax.ppermute(cells, axis, pairs)  8.68 us
    sub x1, other arithmetic, per_device(): fields - (east_flux - west_flux)  4.66 us
    slice x1, local copies, waits for them, and re-layouts, per_device(): fields[:, :, -1]  2.47 us
    slice x1, local copies, waits for them, and re-layouts, per_device(): fields[:, :, :-1]  2.4 us
    unnamed x14, local copies, waits for them, and re-layouts  2.35 us
    slice x1, local copies, waits for them, and re-layouts, per_device(): fields[:, :-1, :]  2.11 us
  transfers between devices with their start and end apart: 4, of which 0 were waited for; matrix products, arithmetic and copies ran while one was open for 17% of the time, Pallas kernels for 0%

profile of v1, /device:TPU:0, one launch (start us, length us, event | category | flops | bytes accessed | tf_op | source)
XLA Modules:
  0.0 83.7 jit_solution(6532169881289247358)
XLA Ops:
  0.0 2.5 %fusion.14 = (f32[5,240,1]{2,1,0:T(8,128)}, f32[5,240,1]{2,1,0:T(8,128)S(1)}) fusion(f32[5,240,360]{2,1,0:T(8,128)} %param.8), kind=kLoop, calls=%fused_computation.41 | loop fusion | bytes 19200 | tf_op jit(solution)/shard_map/slice | solution.py:270
  2.5 1.4 %copy.36 = f32[5,240,1]{1,0,2:T(8,128)S(1)} copy(f32[5,240,1]{2,1,0:T(8,128)} %get-tuple-element.13) | data formatting | bytes 9600
  3.9 0.2 slice_reduce_fusion
  4.1 0.6 collective-permute-start.1
  4.7 4.5 %collective-permute-start.3 = (f32[6,360]{1,0:T(8,128)S(1)}, f32[6,360]{1,0:T(8,128)S(1)}, u32[]{:S(2)}, u32[]{:S(2)}) collective-permute-start(f32[6,360]{1,0:T(8,128)S(1)} %pad_maximum_fusion.2), channel_id=1, source_target_pairs={{0,8},{8,16},{16,24},{1,9},{9,17},{17,25},{2,10},{10,18},{18,26},{... | collective-permute-start | bytes 25928 | tf_op jit(solution)/shard_map/ppermute | solution.py:262
  9.2 0.3 copy.35
  9.5 2.4 %collective-permute-start = (f32[5,240]{1,0:T(8,128)S(1)}, f32[5,240]{1,0:T(8,128)S(1)}, u32[]{:S(2)}, u32[]{:S(2)}) collective-permute-start(f32[5,240]{1,0:T(8,128)S(1)} %bitcast.33), channel_id=1, source_target_pairs={{0,7},{1,0},{2,1},{3,2},{4,3},{5,4},{6,5},{7,6},{8,15},{9,8},{10,9... | collective-permute-start | bytes 14408 | tf_op jit(solution)/shard_map/ppermute | solution.py:262
  11.9 0.6 copy.42
  12.5 1.3 %collective-permute-start.2 = (f32[5,360]{1,0:T(8,128)}, f32[5,360]{1,0:T(8,128)}, u32[]{:S(2)}, u32[]{:S(2)}) collective-permute-start(f32[5,360]{1,0:T(8,128)} %bitcast.22), channel_id=1, source_target_pairs={{8,0},{16,8},{24,16},{9,1},{17,9},{25,17},{10,2},{18,10},{26,18},{... | collective-permute-start | bytes 21608 | tf_op jit(solution)/shard_map/ppermute | solution.py:262
  13.8 0.6 compare_select_fusion
  14.4 0.6 multiply_sine_fusion
  15.1 2.1 %fusion.13 = (f32[5,239,360]{2,1,0:T(8,128)}, f32[5,239,360]{2,1,0:T(8,128)}) fusion(f32[5,240,360]{2,1,0:T(8,128)S(1)} %copy-done.1), kind=kLoop, calls=%fused_computation.40 | loop fusion | bytes 6883200 | tf_op jit(solution)/shard_map/slice | solution.py:280
  17.2 2.4 %fusion.15 = (f32[5,240,359]{2,1,0:T(8,128)}, f32[5,240,359]{2,1,0:T(8,128)}) fusion(f32[5,240,360]{2,1,0:T(8,128)S(1)} %copy-done.1), kind=kLoop, calls=%fused_computation.42 | loop fusion | bytes 6892800 | tf_op jit(solution)/shard_map/slice | solution.py:277
  19.6 0.1 broadcast_compare_fusion.1
  19.7 0.8 dynamic_slice.17
  20.5 0.8 dynamic_slice.19
  21.4 0.1 eq.15
  21.5 0.7 fusion.11
  22.1 0.1 pad_dynamic-slice_fusion.1
  22.3 0.8 copy.33.cut_ref
  23.1 0.8 copy.34.damp_ref
  23.8 0.2 copy.25
  24.1 0.1 copy.27
  24.2 0.9 %broadcast_compare_fusion.2 = (pred[240,360]{1,0:T(8,128)(4,1)}, f32[240,360]{1,0:T(8,128)}) fusion(f32[240,359]{1,0:T(8,128)S(1)} %bitcast.29, f32[240,1]{1,0:T(8,128)S(1)} %copy.27), kind=kLoop, calls=%fused_computation.22 | loop fusion | flops 172800 | bytes 777600 | tf_op jit(solution)/shard_map/gt | solution.py:283
  25.2 1.1 %copy.28 = f32[5,240,1]{2,1,0:T(8,128)} copy(f32[5,240,1]{1,0,2:T(8,128)S(1)} %slice_bitcast_fusion.1) | data formatting | bytes 9600 | tf_op jit(solution)/shard_map/broadcast_in_dim | solution.py:277
  26.3 0.7 copy.30
  27.0 0.1 broadcast_compare_fusion
  27.1 4.7 %fusion.3 = f32[5,240,360]{2,1,0:T(8,128)S(1)} fusion(f32[5,240,360]{2,1,0:T(8,128)S(1)} %copy-done.1, f32[5,240,1]{2,1,0:T(8,128)S(1)} %copy.25, f32[5,240,359]{2,1,0:T(8,128)} %get-tuple-element.16, f32[5,240,359]{2,1,0:T(8,128)} %get-tuple-element.15, f32[5,240,1]{2,1,0:T(8,128)} %copy.28, f32[5,1,360]{2,1,0:T(1,128)S(1)} %copy.30, ...), kind=kLoop, calls=%fused_computation.4 | loop fusion | flops 8208000 | bytes 12098880 | tf_op jit(solution)/shard_map/sub | solution.py:293
  31.8 1.4 %pad.12 = f32[1216,384]{1,0:T(8,128)} pad(f32[1200,360]{1,0:T(8,128)S(1)} %bitcast.25, f32[]{:T(128)} %constant.8.clone.1), padding=0_16x0_24 | pad | bytes 3595780 | tf_op jit(solution)/shard_map/jit(_pad)/pad | solution.py:229
  33.2 47.3 %shard_map.82 = f32[8,152,384]{2,1,0:T(8,128)} custom-call(f32[8,152,384]{2,1,0:T(8,128)} %bitcast.26, s32[152,1]{1,0:T(8,128)} %copy.33.cut_ref, f32[152,1]{1,0:T(8,128)} %copy.34.damp_ref, bf16[1152,768]{1,0:T(8,128)(2,1)} %constant.42.clone.weight, f32[10,384]{1,0:T(8,128)} %constant.43.clone.twiddle), custom_call_target="tpu_custom_call" | custom-call | tf_op jit(solution)/shard_map/pallas_call | solution.py:241
  80.5 1.6 %slice.72 = f32[1200,360]{1,0:T(8,128)S(1)} slice(f32[1216,384]{1,0:T(8,128)} %bitcast.27), slice={[0:1200], [0:360]} | slice | bytes 3456000 | tf_op jit(solution)/shard_map/slice | solution.py:256
  82.2 1.5 %broadcast_select_fusion = f32[5,240,360]{2,1,0:T(8,128)} fusion(f32[5,240,360]{2,1,0:T(8,128)S(1)} %bitcast.28, f32[5,240,360]{2,1,0:T(8,128)S(1)} %fusion.3, pred[240]{0:T(512)(128)(4,1)S(1)} %copy-done.4), kind=kLoop, calls=%fused_computation.15 | loop fusion | flops 432000 | bytes 5184240 | tf_op jit(solution)/shard_map/jit(_where)/select_n | solution.py:299
  (30 shorter events, 0.3 us)
Async XLA Ops:
  0.0 21.4 %copy-start = (s32[4,4,60]{2,1,0:T(4,128)S(1)}, s32[4,4,60]{2,1,0:T(4,128)}, u32[]{:S(2)}) copy-start(s32[4,4,60]{2,1,0:T(4,128)} %param.13) | copy-start | bytes 11524
  0.0 4.6 %copy-start.1 = (f32[5,240,360]{2,1,0:T(8,128)S(1)}, f32[5,240,360]{2,1,0:T(8,128)}, u32[]{:S(2)}) copy-start(f32[5,240,360]{2,1,0:T(8,128)} %param.8) | copy-start | bytes 5184004
  0.0 3.9 %copy-start.2 = (f32[240,360]{1,0:T(8,128)S(1)}, f32[240,360]{1,0:T(8,128)}, u32[]{:S(2)}) copy-start(f32[240,360]{1,0:T(8,128)} %param.9) | copy-start | bytes 1036804
  0.0 4.7 %copy-start.3 = (f32[240,360]{1,0:T(8,128)S(1)}, f32[240,360]{1,0:T(8,128)}, u32[]{:S(2)}) copy-start(f32[240,360]{1,0:T(8,128)} %param.10) | copy-start | bytes 1036804
  4.1 20.0 %collective-permute-start.1 = (f32[6,240]{1,0:T(8,128)S(1)}, f32[6,240]{1,0:T(8,128)S(1)}, u32[]{:S(2)}, u32[]{:S(2)}) collective-permute-start(f32[6,240]{1,0:T(8,128)S(1)} %pad_maximum_fusion.3), channel_id=1, source_target_pairs={{0,1},{1,2},{2,3},{3,4},{4,5},{5,6},{6,7},{7,0},{8,9},{9,10},{10,1... | collective-permute-start | bytes 17288 | tf_op jit(solution)/shard_map/ppermute | solution.py:262
  4.7 22.3 %collective-permute-start.3 = (f32[6,360]{1,0:T(8,128)S(1)}, f32[6,360]{1,0:T(8,128)S(1)}, u32[]{:S(2)}, u32[]{:S(2)}) collective-permute-start(f32[6,360]{1,0:T(8,128)S(1)} %pad_maximum_fusion.2), channel_id=1, source_target_pairs={{0,8},{8,16},{16,24},{1,9},{9,17},{17,25},{2,10},{10,18},{18,26},{... | collective-permute-start | bytes 25928 | tf_op jit(solution)/shard_map/ppermute | solution.py:262
  9.5 14.3 %collective-permute-start = (f32[5,240]{1,0:T(8,128)S(1)}, f32[5,240]{1,0:T(8,128)S(1)}, u32[]{:S(2)}, u32[]{:S(2)}) collective-permute-start(f32[5,240]{1,0:T(8,128)S(1)} %bitcast.33), channel_id=1, source_target_pairs={{0,7},{1,0},{2,1},{3,2},{4,3},{5,4},{6,5},{7,6},{8,15},{9,8},{10,9... | collective-permute-start | bytes 14408 | tf_op jit(solution)/shard_map/ppermute | solution.py:262
  12.5 13.8 %collective-permute-start.2 = (f32[5,360]{1,0:T(8,128)}, f32[5,360]{1,0:T(8,128)}, u32[]{:S(2)}, u32[]{:S(2)}) collective-permute-start(f32[5,360]{1,0:T(8,128)} %bitcast.22), channel_id=1, source_target_pairs={{8,0},{16,8},{24,16},{9,1},{17,9},{25,17},{10,2},{18,10},{26,18},{... | collective-permute-start | bytes 21608 | tf_op jit(solution)/shard_map/ppermute | solution.py:262
  80.5 1.6 %copy-start.4 = (pred[240]{0:T(512)(128)(4,1)S(1)}, pred[240]{0:T(512)(128)(4,1)}, u32[]{:S(2)}) copy-start(pred[240]{0:T(512)(128)(4,1)} %fusion.11) | copy-start | bytes 724

commit v2 on v1

--- a/solution.py
+++ b/solution.py
@@ -163,20 +163,171 @@
     return real_idft(spectrum)
 
 
-def filter_kernel(
-    segments, length, chunks,
-    advected, cut_ref, damp_ref, weight, twiddle, out_ref,
-    gathered, results, spread, send_a, recv_a, send_b, recv_b,
+def spans(start, count, rows_dev, channels):
+    pieces, at, end = [], start, min(start + count, channels * rows_dev)
+    while at < end:
+        channel, row = divmod(at, rows_dev)
+        take = min(end - at, rows_dev - row)
+        pieces.append((at - start, channel, row, take))
+        at += take
+    return pieces
+
+
+def pad_lanes(value, width):
+    rows, length = value.shape
+    if width == length:
+        return value
+    return jnp.concatenate([value, jnp.zeros((rows, width - length), value.dtype)], axis=1)
+
+
+def step_kernel(
+    segments, bands, chunks, share,
+    fields_hbm, east_hbm, north_hbm, cutoff, damping, ship, weight_hbm, twiddle, out_ref,
+    cells, east, north, weight, facts, edge_out, edge_in, advected, gathered, results,
+    returned, spread, cut_ref, damp_ref, polar,
+    load_sem, halo_send, halo_recv, send_a, recv_a, send_b, recv_b,
 ):
-    me = lax.axis_index("lon")
+    channels, rows_dev, length = fields_hbm.shape
+    width = advected.shape[2]
+    lat_count = rows_dev * bands
+    body = pl.ds(8, rows_dev)
+    me, band = lax.axis_index("lon"), lax.axis_index("lat")
+    right, left = lax.rem(me + 1, segments), lax.rem(me + segments - 1, segments)
     peers = [lax.rem(me + p, segments) for p in range(1, segments)]
+    loads = [
+        pltpu.make_async_copy(fields_hbm, cells.at[:, body], load_sem.at[0]),
+        pltpu.make_async_copy(north_hbm, north.at[body], load_sem.at[1]),
+        pltpu.make_async_copy(east_hbm, east, load_sem.at[2]),
+        pltpu.make_async_copy(weight_hbm, weight, load_sem.at[3]),
+    ]
+    for load in loads:
+        load.start()
     barrier = pltpu.get_barrier_semaphore()
     for peer in peers:
         pl.semaphore_signal(barrier, inc=1, device_id={"lon": peer}, device_id_type=MESH)
-    pl.semaphore_wait(barrier, segments - 1)
+
+    @pl.when(band > 0)
+    def _():
+        pl.semaphore_signal(barrier, inc=1, device_id={"lat": band - 1}, device_id_type=MESH)
+
+    @pl.when(band < bands - 1)
+    def _():
+        pl.semaphore_signal(barrier, inc=1, device_id={"lat": band + 1}, device_id_type=MESH)
+
+    @pl.when(band == 0)
+    def _():
+        cells[:, 0:8, :] = jnp.zeros((channels, 8, length), jnp.float32)
+        north[0:8, :] = jnp.zeros((8, length), jnp.float32)
+
+    @pl.when(band == bands - 1)
+    def _():
+        cells[:, rows_dev + 8 : rows_dev + 16, :] = jnp.zeros((channels, 8, length), jnp.float32)
+
+    row = band * rows_dev + lax.broadcasted_iota(jnp.int32, (rows_dev, 128), 0)
+    lane = lax.broadcasted_iota(jnp.int32, (rows_dev, 128), 1)
+    shift = jnp.where(lane == 0, 1.0, jnp.where(lane == 1, 0.0, 0.5))
+    facts[...] = jnp.sin((row.astype(jnp.float32) + shift) * (math.pi / lat_count))
+
+    for load in loads[:3]:
+        load.wait()
+    for c in range(channels):
+        edge_out[0, :, c : c + 1] = cells[c, body, length - 1 : length]
+        edge_out[1, :, c : c + 1] = cells[c, body, 0:1]
+    edge_out[0, :, channels : channels + 1] = east[:, length - 1 : length]
+    beside = jnp.where(band > 0, 1, 0) + jnp.where(band < bands - 1, 1, 0)
+    pl.semaphore_wait(barrier, segments - 1 + beside)
+
+    def halo(source, target, slot, place):
+        return pltpu.make_async_remote_copy(
+            src_ref=source, dst_ref=target, send_sem=halo_send.at[slot],
+            recv_sem=halo_recv.at[slot], device_id=place, device_id_type=MESH,
+        )
+
+    first, last = pl.ds(8, 8), pl.ds(rows_dev, 8)
+    above = pl.ds(rows_dev + 8, 8)
+    up = {"lat": jnp.minimum(band + 1, bands - 1)}
+    down = {"lat": jnp.maximum(band - 1, 0)}
+    northward = [
+        halo(cells.at[:, last], cells.at[:, pl.ds(0, 8)], 0, up),
+        halo(north.at[last], north.at[pl.ds(0, 8)], 1, up),
+    ]
+    southward = halo(cells.at[:, first], cells.at[:, above], 2, down)
+    sideways = [
+        halo(edge_out.at[0], edge_in.at[0], 3, {"lon": right}),
+        halo(edge_out.at[1], edge_in.at[1], 4, {"lon": left}),
+    ]
+    for copy in sideways:
+        copy.start()
+
+    @pl.when(band < bands - 1)
+    def _():
+        for copy in northward:
+            copy.start()
+
+    @pl.when(band > 0)
+    def _():
+        southward.start()
+
+    flat = me * share + lax.broadcasted_iota(jnp.int32, (share, lat_count), 0)
+    wanted = band * rows_dev + lax.rem(flat, rows_dev)
+    hit = wanted == lax.broadcasted_iota(jnp.int32, (share, lat_count), 1)
+    cut_ref[...] = jnp.sum(jnp.where(hit, cutoff[...].astype(jnp.float32), 0.0), axis=1, keepdims=True)
+    damp_ref[...] = jnp.sum(jnp.where(hit, damping[...], 0.0), axis=1, keepdims=True)
+    listed = ship[pl.ds(band, 1), :]
+    own = lax.broadcasted_iota(jnp.int32, (rows_dev, listed.shape[1]), 0)
+    polar[...] = jnp.sum(jnp.where(own == listed, 1.0, 0.0), axis=1, keepdims=True)
+    spread[...] = jnp.zeros_like(spread)
+    for j in range(segments):
+        filled = min(max(channels * rows_dev - j * share, 0), share)
+        if filled < share:
+            advected[j, filled:share, :] = jnp.zeros((share - filled, width), jnp.float32)
+
+    for copy in sideways:
+        copy.wait()
+
+    @pl.when(band < bands - 1)
+    def _():
+        for copy in northward:
+            copy.wait_send()
+        southward.wait_recv()
+
+    @pl.when(band > 0)
+    def _():
+        southward.wait_send()
+        for copy in northward:
+            copy.wait_recv()
+
+    def advect(channel, r, rows):
+        here = pl.ds(r, rows)
+        field = pad_lanes(cells[channel, pl.ds(r + 8, rows), :], width)
+        upper = pad_lanes(cells[channel, pl.ds(r + 9, rows), :], width)
+        lower = pad_lanes(cells[channel, pl.ds(r + 7, rows), :], width)
+        courant_e = pad_lanes(east[here, :], width)
+        courant_n = pad_lanes(north[pl.ds(r + 8, rows), :], width)
+        courant_s = pad_lanes(north[pl.ds(r + 7, rows), :], width)
+        column = lax.broadcasted_iota(jnp.int32, (rows, width), 1)
+        grow = band * rows_dev + r + lax.broadcasted_iota(jnp.int32, (rows, 1), 0)
+        east_cell = edge_in[1, here, channel : channel + 1]
+        west_cell = edge_in[0, here, channel : channel + 1]
+        west_courant = edge_in[0, here, channels : channels + 1]
+        ahead = jnp.where(column == length - 1, east_cell, pltpu.roll(field, width - 1, 1))
+        east_flux = courant_e * jnp.where(courant_e > 0, field, ahead)
+        entering = west_courant * jnp.where(west_courant > 0, west_cell, field[:, 0:1])
+        west_flux = jnp.where(column == 0, entering, pltpu.roll(east_flux, 1, 1))
+        west_flux = jnp.where(column < length, west_flux, 0.0)
+        face_n, face_s = facts[here, 0:1], facts[here, 1:2]
+        north_flux = courant_n * jnp.where(courant_n > 0, field, upper) * face_n
+        south_flux = courant_s * jnp.where(courant_s > 0, lower, field) * face_s
+        north_flux = jnp.where(grow < lat_count - 1, north_flux, 0.0)
+        south_flux = jnp.where(grow > 0, south_flux, 0.0)
+        return field - (east_flux - west_flux) - (north_flux - south_flux) * (1.0 / facts[here, 2:3])
+
     outward, homeward = [], []
     for c, (start, rows) in enumerate(chunks):
         window = pl.ds(start, rows)
+        for j in range(segments):
+            for offset, channel, r, count in spans(j * share + start, rows, rows_dev, channels):
+                advected[j, start + offset : start + offset + count, :] = advect(channel, r, count)
         for p, peer in enumerate(peers):
             copy = pltpu.make_async_remote_copy(
                 src_ref=advected.at[peer, window],
@@ -188,6 +339,7 @@
             )
             copy.start()
             outward.append(copy)
+    loads[3].wait()
     for c, (start, rows) in enumerate(chunks):
         window = pl.ds(start, rows)
         gathered[me, window] = advected[me, window]
@@ -195,14 +347,15 @@
             outward[c * (segments - 1) + p].wait_recv()
         filtered = filter_rows(
             [gathered[j, window] for j in range(segments)],
-            cut_ref[window, :], damp_ref[window, :], weight, twiddle, spread, length,
+            cut_ref[window, :].astype(jnp.int32), damp_ref[window, :], weight, twiddle, spread,
+            length,
         )
         for j in range(segments):
             results[j, window] = filtered[j]
         for p, peer in enumerate(peers):
             copy = pltpu.make_async_remote_copy(
                 src_ref=results.at[peer, window],
-                dst_ref=out_ref.at[me, window],
+                dst_ref=returned.at[me, window],
                 send_sem=send_b.at[c, p],
                 recv_sem=recv_b.at[c, p],
                 device_id={"lon": peer},
@@ -210,97 +363,64 @@
             )
             copy.start()
             homeward.append(copy)
-        out_ref[me, window] = results[me, window]
-    for copy in outward:
+        returned[me, window] = results[me, window]
+    for c, (start, rows) in enumerate(chunks):
+        for p in range(segments - 1):
+            homeward[c * (segments - 1) + p].wait_recv()
+        for j in range(segments):
+            for offset, channel, r, count in spans(j * share + start, rows, rows_dev, channels):
+                here = slice(start + offset, start + offset + count)
+                chosen = jnp.where(polar[r : r + count, :] > 0.0, returned[j, here, :], advected[j, here, :])
+                out_ref[channel, r : r + count, :] = chosen[:, :length]
+    for copy in outward + homeward:
         copy.wait_send()
-    for copy in homeward:
-        copy.wait()
-
-
-def circle_filter(advected, cut_rows, damp_rows, pieces=3):
-    segments = lax.axis_size("lon")
-    channels, rows_dev, length = advected.shape
+
+
+def per_device(pieces, fields, east_courant, north_courant, cutoff, damping, ship_rows):
+    channels, rows_dev, length = fields.shape
+    segments, bands = lax.axis_size("lon"), lax.axis_size("lat")
     width = ceil_to(length, 128)
     share = ceil_to(ceil_to(channels * rows_dev, segments) // segments, 8)
-    padded = share * segments
     chunks = chunk_rows(share, pieces)
     weight, twiddle = tables(segments, length, width)
-    slots = segments + 2
-    flat = jnp.pad(
-        advected.reshape(channels * rows_dev, length),
-        ((0, padded - channels * rows_dev), (0, width - length)),
-    ).reshape(segments, share, width)
-    me = lax.axis_index("lon")
-
-    def mine(values):
-        column = jnp.pad(jnp.tile(values, channels), (0, padded - channels * rows_dev))
-        return lax.dynamic_slice_in_dim(column, me * share, share)[:, None]
-
-    depth = slots * ceil_to(max(rows for _, rows in chunks), 16)
+    depth = (segments + 2) * ceil_to(max(rows for _, rows in chunks), 16)
     semaphores = pltpu.SemaphoreType.DMA((len(chunks), segments - 1))
-    filtered = pl.pallas_call(
-        functools.partial(filter_kernel, segments, length, chunks),
-        out_shape=jax.ShapeDtypeStruct((segments, share, width), jnp.float32),
-        in_specs=[pl.BlockSpec(memory_space=pltpu.VMEM)] * 5,
-        out_specs=pl.BlockSpec(memory_space=pltpu.VMEM),
+    block = pltpu.VMEM((segments, share, width), jnp.float32)
+    whole, local = pl.BlockSpec(memory_space=pl.ANY), pl.BlockSpec(memory_space=pltpu.VMEM)
+    return pl.pallas_call(
+        functools.partial(step_kernel, segments, bands, chunks, share),
+        out_shape=jax.ShapeDtypeStruct(fields.shape, jnp.float32),
+        in_specs=[whole, whole, whole, local, local, local, whole, local],
+        out_specs=local,
         scratch_shapes=[
-            pltpu.VMEM((segments, share, width), jnp.float32),
-            pltpu.VMEM((segments, share, width), jnp.float32),
+            pltpu.VMEM((channels, rows_dev + 16, length), jnp.float32),
+            pltpu.VMEM((rows_dev, length), jnp.float32),
+            pltpu.VMEM((rows_dev + 16, length), jnp.float32),
+            pltpu.VMEM(weight.shape, BF16),
+            pltpu.VMEM((rows_dev, 128), jnp.float32),
+            pltpu.VMEM((2, rows_dev, 128), jnp.float32),
+            pltpu.VMEM((2, rows_dev, 128), jnp.float32),
+            block, block, block, block,
             pltpu.VMEM((depth, 3 * width), BF16),
+            pltpu.VMEM((share, 1), jnp.float32),
+            pltpu.VMEM((share, 1), jnp.float32),
+            pltpu.VMEM((rows_dev, 1), jnp.float32),
+            pltpu.SemaphoreType.DMA((4,)),
+            pltpu.SemaphoreType.DMA((5,)),
+            pltpu.SemaphoreType.DMA((5,)),
             semaphores, semaphores, semaphores, semaphores,
         ],
         compiler_params=pltpu.CompilerParams(
             collective_id=0, has_side_effects=True, vmem_limit_bytes=56 * 1024 * 1024
         ),
-    )(flat, mine(cut_rows), mine(damp_rows), jnp.asarray(weight), jnp.asarray(twiddle))
-    return filtered.reshape(padded, width)[: channels * rows_dev, :length].reshape(advected.shape)
-
-
-def shifted(cells, axis, step, closed):
-    count = lax.axis_size(axis)
-    pairs = [(i, (i + step) % count) for i in range(count) if closed or 0 <= i + step < count]
-    return lax.ppermute(cells, axis, pairs)
-
-
-def per_device(fields, east_courant, north_courant, cutoff, damping, ship_rows):
-    channels, rows_dev, length = fields.shape
-    bands = lax.axis_size("lat")
-    lat_count = rows_dev * bands
-    band = lax.axis_index("lat")
-    stacked_east = jnp.concatenate([fields[:, :, -1], east_courant[None, :, -1]], axis=0)
-    west_edge = shifted(stacked_east, "lon", 1, True)
-    east_edge = shifted(fields[:, :, 0], "lon", -1, True)
-    stacked_north = jnp.concatenate([fields[:, -1, :], north_courant[None, -1, :]], axis=0)
-    south_edge = shifted(stacked_north, "lat", 1, False)
-    north_edge = shifted(fields[:, 0, :], "lat", -1, False)
-    east_cells = jnp.concatenate([fields[:, :, 1:], east_edge[:, :, None]], axis=2)
-    west_cells = jnp.concatenate([west_edge[:channels, :, None], fields[:, :, :-1]], axis=2)
-    west_courant = jnp.concatenate([west_edge[channels, :, None], east_courant[:, :-1]], axis=1)
-    north_cells = jnp.concatenate([fields[:, 1:, :], north_edge[:, None, :]], axis=1)
-    south_cells = jnp.concatenate([south_edge[:channels, None, :], fields[:, :-1, :]], axis=1)
-    south_courant = jnp.concatenate([south_edge[channels, None, :], north_courant[:-1]], axis=0)
-    east_flux = east_courant * jnp.where(east_courant > 0, fields, east_cells)
-    west_flux = west_courant * jnp.where(west_courant > 0, west_cells, fields)
-    global_rows = band * rows_dev + jnp.arange(rows_dev, dtype=jnp.int32)
-    latitudes = global_rows.astype(jnp.float32)
-    face_n = jnp.sin((latitudes + 1.0) * (math.pi / lat_count))
-    face_s = jnp.sin(latitudes * (math.pi / lat_count))
-    centre = jnp.sin((latitudes + 0.5) * (math.pi / lat_count))
-    face_n = jnp.where(global_rows < lat_count - 1, face_n, 0.0)
-    face_s = jnp.where(global_rows > 0, face_s, 0.0)
-    north_flux = north_courant * jnp.where(north_courant > 0, fields, north_cells) * face_n[:, None]
-    south_flux = south_courant * jnp.where(south_courant > 0, south_cells, fields) * face_s[:, None]
-    advected = fields - (east_flux - west_flux) - (north_flux - south_flux) / centre[:, None]
-    cut_rows = lax.dynamic_slice_in_dim(cutoff, band * rows_dev, rows_dev)
-    damp_rows = lax.dynamic_slice_in_dim(damping, band * rows_dev, rows_dev)
-    listed = lax.dynamic_index_in_dim(ship_rows, band, axis=0, keepdims=False).reshape(-1)
-    polar = jnp.any(listed[:, None] == jnp.arange(rows_dev, dtype=jnp.int32)[None, :], axis=0)
-    filtered = circle_filter(advected, cut_rows, damp_rows)
-    return jnp.where(polar[None, :, None], filtered, advected)
+    )(
+        fields, east_courant, north_courant, cutoff[None, :], damping[None, :],
+        ship_rows.reshape(bands, -1), jnp.asarray(weight), jnp.asarray(twiddle),
+    )
 
 
 def solution(mesh):
     placed = (P(None, "lat", "lon"), P("lat", "lon"), P("lat", "lon"), P(), P(), P())
     return jax.shard_map(
-        per_device, mesh=mesh, in_specs=placed, out_specs=P(None, "lat", "lon"), check_vma=False
+        functools.partial(per_device, 3), mesh=mesh, in_specs=placed, out_specs=P(None, "lat", "lon"), check_vma=False
     )

time: 85.2 us -> 59.4 us (0.70)
  local copies, waits for them, and re-layouts: 18.2 us -> 4.22 us
  other arithmetic: 9.29 us -> 0 us
  starting transfers between devices: 8.68 us -> 0 us
  Pallas kernels: 47.3 us -> 54 us
    slice x8 -> x0, local copies, waits for them, and re-layouts: 8.81 us -> none  [the longest x1 2.47 us: per_device(): fields[:, :, -1]]
    ppermute x4 -> x0, starting transfers between devices: 8.68 us -> none  [shifted(): return lax.ppermute(cells, axis, pairs)]
    pallas_call x1, Pallas kernels: 47.3 us -> 54 us  [per_device(): pl.pallas_call(functools.partial(step_kernel, segments, bands, chunks, sh...]
    sub x1 -> x0, other arithmetic: 4.66 us -> none  [per_device(): fields - (east_flux - west_flux)]
    broadcast_in_dim x8 -> x0, local copies, waits for them, and re-layouts: 3.57 us -> none  [the longest x2 1.5 us: mine(): return lax.dynamic_slice_in_dim(column, me * share, share)[:, None]]
    select_n x2 -> x0, other arithmetic: 2.19 us -> none  [the longest x1 1.55 us: per_device(): return jnp.where(polar[None, :, None], filtered, advected)]
    dynamic_slice x5 -> x0, local copies, waits for them, and re-layouts: 1.69 us -> none  [the longest x1 0.77 us: per_device(): cut_rows = lax.dynamic_slice_in_dim(cutoff, band * rows_dev, rows_dev)]
    pad x1 -> x0, local copies, waits for them, and re-layouts: 1.4 us -> none  [circle_filter(): jnp.pad(advected.reshape(channels * rows_dev, length), ((0, padded - chan...]
  transfers between devices with their start and end apart: 4 -> 0, of which waited for: 0 -> 0; matrix products, arithmetic and copies ran while one was open for 17% -> 0% of each run, Pallas kernels for 0% -> 0%
where the time goes in v2:
time: 59.4 us; the launch traced here: 58.2 us
  Pallas kernels  54 us (91%)
  local copies, waits for them, and re-layouts  4.22 us (7%)
    pallas_call x1, Pallas kernels, per_device(): pl.pallas_call(functools.partial(step_kernel, segments, bands, chunks, sh...  54 us
    unnamed x1, local copies, waits for them, and re-layouts  2.85 us
    reshape x1, local copies, waits for them, and re-layouts, per_device(): ship_rows.reshape(bands, -1)  1.37 us

profile of v2, /device:TPU:0, one launch (start us, length us, event | category | flops | bytes accessed | tf_op | source)
XLA Modules:
  0.0 58.2 jit_solution(14285708248978700244)
XLA Ops:
  0.0 1.4 %reshape.3.ship = s32[4,240]{1,0:T(4,128)} reshape(s32[4,4,60]{2,1,0:T(4,128)} %param.13) | data formatting | bytes 7680 | tf_op jit(solution)/shard_map/reshape | solution.py:418
  1.4 54.0 %shard_map.82 = f32[5,240,360]{2,1,0:T(8,128)} custom-call(f32[5,240,360]{2,1,0:T(8,128)} %fields_hbm.1, f32[240,360]{1,0:T(8,128)} %east_hbm.1, f32[240,360]{1,0:T(8,128)} %north_hbm.1, s32[1,960]{1,0:T(1,128)} %bitcast.2, f32[1,960]{1,0:T(1,128)} %bitcast.3, s32[4,240]{1,0:T(4,128)} %reshape.3.ship, bf16[1152,768]{1,0:T(8,128)(2,1)} %constant.4.clone.weight_hbm, ...), custom_call_target="tpu_custom_call" | custom-call | tf_op jit(solution)/shard_map/pallas_call | solution.py:390
  55.4 2.9 %copy.10 = f32[5,240,360]{2,1,0:T(8,128)} copy(f32[5,240,360]{2,1,0:T(8,128)} %shard_map.82) | data formatting | bytes 3456000

commit v3 on v2

--- a/solution.py
+++ b/solution.py
@@ -173,6 +173,20 @@
     return pieces
 
 
+def partners(me, count):
+    bits = count.bit_length() - 1
+    half = count // 2
+    order = [p for q in range(half) for p in (half + (half - 1 - q), q) if p]
+    flipped = []
+    for p in order:
+        other = 0
+        for i in range(bits):
+            bit = lax.rem(me // (1 << i), 2)
+            other = other + (1 << i) * ((1 - bit) if (p >> i) & 1 else bit)
+        flipped.append(other)
+    return flipped
+
+
 def pad_lanes(value, width):
     rows, length = value.shape
     if width == length:
@@ -182,9 +196,9 @@
 
 def step_kernel(
     segments, bands, chunks, share,
-    fields_hbm, east_hbm, north_hbm, cutoff, damping, ship, weight_hbm, twiddle, out_ref,
-    cells, east, north, weight, facts, edge_out, edge_in, advected, gathered, results,
-    returned, spread, cut_ref, damp_ref, polar,
+    fields_hbm, east_hbm, north_hbm, cutoff, damping, ship, weight_hbm, twiddle, out_ref, kept_hbm, polar,
+    cells, kept, east, north, weight, facts, edge_out, edge_in, advected, gathered, results,
+    returned, spread, cut_ref, damp_ref,
     load_sem, halo_send, halo_recv, send_a, recv_a, send_b, recv_b,
 ):
     channels, rows_dev, length = fields_hbm.shape
@@ -193,7 +207,7 @@
     body = pl.ds(8, rows_dev)
     me, band = lax.axis_index("lon"), lax.axis_index("lat")
     right, left = lax.rem(me + 1, segments), lax.rem(me + segments - 1, segments)
-    peers = [lax.rem(me + p, segments) for p in range(1, segments)]
+    peers = partners(me, segments)
     loads = [
         pltpu.make_async_copy(fields_hbm, cells.at[:, body], load_sem.at[0]),
         pltpu.make_async_copy(north_hbm, north.at[body], load_sem.at[1]),
@@ -273,9 +287,12 @@
     hit = wanted == lax.broadcasted_iota(jnp.int32, (share, lat_count), 1)
     cut_ref[...] = jnp.sum(jnp.where(hit, cutoff[...].astype(jnp.float32), 0.0), axis=1, keepdims=True)
     damp_ref[...] = jnp.sum(jnp.where(hit, damping[...], 0.0), axis=1, keepdims=True)
-    listed = ship[pl.ds(band, 1), :]
-    own = lax.broadcasted_iota(jnp.int32, (rows_dev, listed.shape[1]), 0)
-    polar[...] = jnp.sum(jnp.where(own == listed, 1.0, 0.0), axis=1, keepdims=True)
+    own = lax.broadcasted_iota(jnp.int32, (rows_dev, ship.shape[2]), 0)
+    lists = ship[band]
+    found = jnp.zeros(own.shape, jnp.float32)
+    for d in range(bands):
+        found += jnp.where(own == lists[d : d + 1, :], 1.0, 0.0)
+    polar[...] = jnp.sum(found, axis=1, keepdims=True)
     spread[...] = jnp.zeros_like(spread)
     for j in range(segments):
         filled = min(max(channels * rows_dev - j * share, 0), share)
@@ -327,7 +344,9 @@
         window = pl.ds(start, rows)
         for j in range(segments):
             for offset, channel, r, count in spans(j * share + start, rows, rows_dev, channels):
-                advected[j, start + offset : start + offset + count, :] = advect(channel, r, count)
+                value = advect(channel, r, count)
+                advected[j, start + offset : start + offset + count, :] = value
+                kept[channel, r : r + count, :] = value[:, :length]
         for p, peer in enumerate(peers):
             copy = pltpu.make_async_remote_copy(
                 src_ref=advected.at[peer, window],
@@ -339,6 +358,8 @@
             )
             copy.start()
             outward.append(copy)
+    keep = pltpu.make_async_copy(kept, kept_hbm, load_sem.at[4])
+    keep.start()
     loads[3].wait()
     for c, (start, rows) in enumerate(chunks):
         window = pl.ds(start, rows)
@@ -370,10 +391,10 @@
         for j in range(segments):
             for offset, channel, r, count in spans(j * share + start, rows, rows_dev, channels):
                 here = slice(start + offset, start + offset + count)
-                chosen = jnp.where(polar[r : r + count, :] > 0.0, returned[j, here, :], advected[j, here, :])
-                out_ref[channel, r : r + count, :] = chosen[:, :length]
+                out_ref[channel, r : r + count, :] = returned[j, here, :][:, :length]
     for copy in outward + homeward:
         copy.wait_send()
+    keep.wait()
 
 
 def per_device(pieces, fields, east_courant, north_courant, cutoff, damping, ship_rows):
@@ -387,13 +408,18 @@
     semaphores = pltpu.SemaphoreType.DMA((len(chunks), segments - 1))
     block = pltpu.VMEM((segments, share, width), jnp.float32)
     whole, local = pl.BlockSpec(memory_space=pl.ANY), pl.BlockSpec(memory_space=pltpu.VMEM)
-    return pl.pallas_call(
+    filtered, advected, polar = pl.pallas_call(
         functools.partial(step_kernel, segments, bands, chunks, share),
-        out_shape=jax.ShapeDtypeStruct(fields.shape, jnp.float32),
+        out_shape=[
+            jax.ShapeDtypeStruct(fields.shape, jnp.float32),
+            jax.ShapeDtypeStruct(fields.shape, jnp.float32),
+            jax.ShapeDtypeStruct((rows_dev, 1), jnp.float32),
+        ],
         in_specs=[whole, whole, whole, local, local, local, whole, local],
-        out_specs=local,
+        out_specs=[local, whole, local],
         scratch_shapes=[
             pltpu.VMEM((channels, rows_dev + 16, length), jnp.float32),
+            pltpu.VMEM(fields.shape, jnp.float32),
             pltpu.VMEM((rows_dev, length), jnp.float32),
             pltpu.VMEM((rows_dev + 16, length), jnp.float32),
             pltpu.VMEM(weight.shape, BF16),
@@ -404,8 +430,7 @@
             pltpu.VMEM((depth, 3 * width), BF16),
             pltpu.VMEM((share, 1), jnp.float32),
             pltpu.VMEM((share, 1), jnp.float32),
-            pltpu.VMEM((rows_dev, 1), jnp.float32),
-            pltpu.SemaphoreType.DMA((4,)),
+            pltpu.SemaphoreType.DMA((5,)),
             pltpu.SemaphoreType.DMA((5,)),
             pltpu.SemaphoreType.DMA((5,)),
             semaphores, semaphores, semaphores, semaphores,
@@ -415,12 +440,13 @@
         ),
     )(
         fields, east_courant, north_courant, cutoff[None, :], damping[None, :],
-        ship_rows.reshape(bands, -1), jnp.asarray(weight), jnp.asarray(twiddle),
+        ship_rows, jnp.asarray(weight), jnp.asarray(twiddle),
     )
+    return jnp.where(polar[None] > 0.0, filtered, advected)
 
 
 def solution(mesh):
     placed = (P(None, "lat", "lon"), P("lat", "lon"), P("lat", "lon"), P(), P(), P())
     return jax.shard_map(
-        functools.partial(per_device, 3), mesh=mesh, in_specs=placed, out_specs=P(None, "lat", "lon"), check_vma=False
+        functools.partial(per_device, 5), mesh=mesh, in_specs=placed, out_specs=P(None, "lat", "lon"), check_vma=False
     )

time: 59.4 us -> 60.4 us (1.017); the launches traced: 58.2 us -> 60.2 us
  other arithmetic: 0 us -> 4.55 us
  local copies, waits for them, and re-layouts: 4.22 us -> 0 us
  Pallas kernels: 54 us -> 55.6 us
    select_n x0 -> x1, other arithmetic: none -> 3.54 us  [per_device(): return jnp.where(polar[None] > 0.0, filtered, advected)]
    unnamed x1 -> x0, local copies, waits for them, and re-layouts: 2.85 us -> none
    pallas_call x1, Pallas kernels: 54 us -> 55.6 us  [per_device(): pl.pallas_call(functools.partial(step_kernel, segments, bands, chunks, sh...]
    reshape x1 -> x0, local copies, waits for them, and re-layouts: 1.37 us -> none  [per_device(): ship_rows.reshape(bands, -1)]
    gt x0 -> x1, other arithmetic: none -> 1.01 us  [per_device(): return jnp.where(polar[None] > 0.0, filtered, advected)]
where the time goes in v3:
time: 60.4 us; the launch traced here: 60.2 us
  Pallas kernels  55.6 us (92%)
  other arithmetic  4.55 us (8%)
    pallas_call x1, Pallas kernels, per_device(): pl.pallas_call(functools.partial(step_kernel, segments, bands, chunks, sh...  55.6 us
    select_n x1, other arithmetic, per_device(): return jnp.where(polar[None] > 0.0, filtered, advected)  3.54 us

profile of v3, /device:TPU:0, one launch (start us, length us, event | category | flops | bytes accessed | tf_op | source)
XLA Modules:
  0.0 60.2 jit_solution(8425014231345591770)
XLA Ops:
  0.0 55.6 %shard_map.82 = (f32[5,240,360]{2,1,0:T(8,128)}, f32[5,240,360]{2,1,0:T(8,128)}, f32[240,1]{1,0:T(8,128)}) custom-call(f32[5,240,360]{2,1,0:T(8,128)} %fields_hbm.1, f32[240,360]{1,0:T(8,128)} %east_hbm.1, f32[240,360]{1,0:T(8,128)} %north_hbm.1, s32[1,960]{1,0:T(1,128)} %bitcast.2, f32[1,960]{1,0:T(1,128)} %bitcast.3, s32[4,4,60]{2,1,0:T(4,128)} %ship.1, ...), custom_call_target="tpu_custom_call" | custom-call | tf_op jit(solution)/shard_map/pallas_call | solution.py:411
  55.6 1.0 %compare_reduce_fusion = pred[240]{0:T(512)(128)(4,1)S(1)} fusion(f32[240,1]{1,0:T(8,128)} %get-tuple-element.8), kind=kLoop, calls=%fused_computation.1 | loop fusion | flops 240 | bytes 1200 | tf_op jit(solution)/shard_map/gt | solution.py:445
  56.7 3.5 %broadcast_select_fusion = f32[5,240,360]{2,1,0:T(8,128)} fusion(f32[5,240,360]{2,1,0:T(8,128)} %get-tuple-element.9, f32[5,240,360]{2,1,0:T(8,128)} %get-tuple-element.10, pred[240]{0:T(512)(128)(4,1)S(1)} %compare_reduce_fusion), kind=kLoop, calls=%fused_computation | loop fusion | flops 432000 | bytes 5184240 | tf_op jit(solution)/shard_map/jit(_where)/select_n | solution.py:445
